TPU v7x, 256 devices: a whole 4x4x8 slice. The times are simulated.
256 devices in a mesh: group: 8 (over x_lo, y), member: 32 (over x_hi, z, core).
Axes of the slice: x: 4 (x_hi: 2, x_lo: 2; x = x_hi * 2 + x_lo), y: 4, z: 8, core: 2. Of those that a mesh axis runs over, the one named last changes fastest.
Arguments:
- entity: bfloat16 [65536, 800], P(('group', 'member')), may hold values from -3 to 7.5
- adagrad_state: float32 [65536], P(('group', 'member')), may hold values from 0.01 to 1
- relation: bfloat16 [1345, 800], replicated, may hold values from -1.8 to 1.8
- source_ids: int32 [2, 131072], P(None, ('group', 'member')), may hold values from 0 to 255
- relation_ids: int32 [2, 131072], P(None, ('group', 'member')), may hold values from 0 to 1344
- dest_groups: int32 [2, 131072, 1], P(None, ('group', 'member')), may hold values from 0 to 7; in each aligned block of 512 rows (0 to 511, 512 to 1023, ..., all dimensions but the last counted through in order) at most 128 rows name the same one
- dest_rows: int32 [2, 131072], P(None, ('group', 'member')), may hold values from 0 to 255
- negative_ids: int32 [2, 256000], P(None, ('group', 'member')), may hold values from 0 to 255
- owners: int32 [2, 8], replicated, may hold values from 0 to 31
Outputs:
- new_entity: bfloat16 [65536, 800], P(('group', 'member'))
- new_state: float32 [65536], P(('group', 'member'))
Inputs may be any that keep to these rules, and one draw needn't show every extreme that they name: `dest_groups`: for each sub-step and each device's 512 edges, at most 128 name any one destination group, a bound that some block reaches.
All inputs are finite; a program needn't handle non-finite values.
Results may differ from a plain program's by a relative error of at most 0.017.
Values may be sent and summed in bfloat16 or wider, within the bound.
A program may use at most 64 MiB of HBM per device.

v0:
```python
import jax
import jax.numpy as jnp
from jax import lax
from jax.sharding import PartitionSpec as P


def broadcast(value, axis, source):
    kept = jnp.where(lax.axis_index(axis) == source, value, 0).astype(value.dtype)
    return lax.psum(kept, axis)


def complex_query(source, rel):
    half = source.shape[-1] // 2
    sr, si = (source[..., :half], source[..., half:])
    rr, ri = (rel[..., :half], rel[..., half:])
    return jnp.concatenate([sr * rr - si * ri, sr * ri + si * rr], -1)


def source_grad(grad_query, rel):
    half = grad_query.shape[-1] // 2
    gr, gi = (grad_query[..., :half], grad_query[..., half:])
    rr, ri = (rel[..., :half], rel[..., half:])
    return jnp.concatenate([gr * rr + gi * ri, gi * rr - gr * ri], -1)


def edge_terms(source_rows, rel_rows, dest_rows, negatives):
    rel = rel_rows.astype(jnp.float32)
    query = complex_query(source_rows.astype(jnp.float32), rel).astype(jnp.bfloat16)
    dest = dest_rows.astype(jnp.float32)
    positive = jnp.sum(query.astype(jnp.float32) * dest, -1)
    scores = lax.dot_general(
        query, negatives, (((1,), (1,)), ((), ())), preferred_element_type=jnp.float32
    )
    top = jnp.maximum(jnp.max(scores, 1), positive)
    pos_exp = jnp.exp(positive - top)
    neg_exp = jnp.exp(scores - top[:, None])
    total = pos_exp + jnp.sum(neg_exp, 1)
    coef_pos = pos_exp / total - 1.0
    coef_neg = (neg_exp / total[:, None]).astype(jnp.bfloat16)
    grad_query = coef_pos[:, None] * dest + jnp.dot(
        coef_neg, negatives, preferred_element_type=jnp.float32
    )
    grad_source = source_grad(grad_query, rel)
    grad_neg = lax.dot_general(
        coef_neg, query, (((0,), (0,)), ((), ())), preferred_element_type=jnp.float32
    )
    return (grad_source, query, coef_pos, grad_neg)


def scatter_rows(values, row_ids, count):
    onehot = (row_ids[:, None] == jnp.arange(count, dtype=jnp.int32)[None, :]).astype(jnp.float32)
    return lax.dot_general(
        onehot,
        values,
        (((0,), (0,)), ((), ())),
        precision=lax.Precision.HIGHEST,
        preferred_element_type=jnp.float32,
    )


def per_device(
    entity,
    adagrad_state,
    relation,
    source_ids,
    relation_ids,
    dest_groups,
    dest_rows,
    negative_ids,
    owners,
):
    groups = lax.axis_size("group")
    group_index = lax.axis_index("group")
    member_index = lax.axis_index("member")
    shard_rows = entity.shape[0]
    table = entity
    state = adagrad_state
    for step in range(source_ids.shape[0]):
        root = owners[step, group_index]
        block = broadcast(table, "member", root)
        src = source_ids[step]
        rel = relation_ids[step]
        dgr = dest_groups[step, :, 0]
        drw = dest_rows[step]
        neg = negative_ids[step]
        source_rows = jnp.take(block, src, axis=0)
        rel_rows = jnp.take(relation, rel, axis=0)
        negatives = jnp.take(table, neg, axis=0)
        whole = lax.all_gather(table, "group", axis=0, tiled=True)
        flat = dgr * shard_rows + drw
        dest_vals = jnp.take(whole, flat, axis=0)
        grad_source, query, coef_pos, grad_neg = edge_terms(
            source_rows, rel_rows, dest_vals, negatives
        )
        grad_dest = coef_pos[:, None] * query.astype(jnp.float32)
        spread = scatter_rows(grad_dest, flat, groups * shard_rows)
        dest_total = lax.psum_scatter(spread, "group", scatter_dimension=0, tiled=True)
        source_part = scatter_rows(grad_source, src, shard_rows)
        source_total = lax.psum(source_part, "member")
        neg_total = scatter_rows(grad_neg, neg, shard_rows)
        grads = dest_total + neg_total + jnp.where(member_index == root, source_total, 0.0)
        state = state + jnp.mean(grads * grads, -1)
        table = (table.astype(jnp.float32) - 1.0 * grads / jnp.sqrt(state)[:, None]).astype(
            jnp.bfloat16
        )
    return (table, state)


def solution(mesh):
    placed = (
        P(("group", "member"), None),
        P(("group", "member")),
        P(),
        P(None, ("group", "member")),
        P(None, ("group", "member")),
        P(None, ("group", "member"), None),
        P(None, ("group", "member")),
        P(None, ("group", "member")),
        P(),
    )
    return jax.shard_map(
        per_device,
        mesh=mesh,
        in_specs=placed,
        out_specs=(P(("group", "member"), None), P(("group", "member"))),
        check_vma=False,
    )
```

profile of v0, /device:TPU:16, one launch (start us, length us, event | category | flops | bytes accessed | tf_op | source)
XLA Modules:
  0.0 1122.0 jit_solution(834115604931892025)
XLA Ops:
  8.1 1.4 constant_dynamic-slice_fusion.1
  11.0 2.0 copy.15
  13.1 0.9 copy-done
  14.0 5.3 gather_fusion.3
  19.3 3.4 copy.13
  22.8 2.1 gather_fusion.1
  24.9 1.3 copy.14
  26.3 246.0 %all-reduce.5.cloned.1.call-done = bf16[256,800]{0,1:T(8,128)(2,1)} async-done(((bf16[256,800]{0,1:T(8,128)(2,1)}), bf16[256,800]{0,1:T(8,128)(2,1)}) %all-reduce.5.cloned.1.call-update) | async-done | bytes 409616 | tf_op jit(solution)/shard_map/psum | solution.py:9
  272.3 1.2 copy.11
  273.5 2.8 gather_fusion
  276.3 2.3 copy.12
  278.5 1.4 select_convert_fusion.2
  282.0 2.6 fusion.44
  284.5 5.0 gather_fusion.2
  289.6 1.3 copy.16
  290.9 1.8 fusion.6
  292.7 1.9 fusion.4
  294.7 3.0 fusion.7
  298.1 1.9 fusion.10
  300.2 7.7 fusion
  308.7 4.7 fusion.38
  313.4 244.1 %all-reduce.7.cloned.1.call-done = f32[256,800]{0,1:T(8,128)} async-done(((f32[256,800]{0,1:T(8,128)}), f32[256,800]{0,1:T(8,128)}) %all-reduce.7.cloned.1.call-update) | async-done | bytes 819216 | tf_op jit(solution)/shard_map/psum | solution.py:99
  557.5 5.4 multiply_reduce_fusion.1
  562.9 1.1 broadcast_select_fusion.8
  564.9 2.1 gather_fusion.5
  567.0 1.3 copy.21
  568.4 1.3 select_convert_fusion
  569.9 5.3 gather_fusion.7
  575.2 243.6 %all-reduce.9.cloned.1.call-done = bf16[256,800]{0,1:T(8,128)(2,1)} async-done(((bf16[256,800]{0,1:T(8,128)(2,1)}), bf16[256,800]{0,1:T(8,128)(2,1)}) %all-reduce.9.cloned.1.call-update) | async-done | bytes 409616 | tf_op jit(solution)/shard_map/psum | solution.py:9
  818.8 1.2 copy.18
  820.0 2.1 gather_fusion.4
  822.1 1.2 copy.19
  823.4 1.3 select_convert_fusion.1
  825.1 1.2 copy-done.12
  826.2 2.6 fusion.45
  828.9 6.0 copy.22
  834.9 5.0 gather_fusion.6
  839.9 1.3 copy.23
  841.2 1.7 fusion.8
  842.9 1.9 fusion.5
  844.9 2.9 fusion.9
  848.1 1.9 fusion.14
  850.4 7.7 fusion.1
  858.1 1.6 copy-done.10
  859.7 3.1 fusion.37
  862.8 244.7 %all-reduce.11.cloned.1.call-done = f32[256,800]{0,1:T(8,128)} async-done(((f32[256,800]{0,1:T(8,128)}), f32[256,800]{0,1:T(8,128)}) %all-reduce.11.cloned.1.call-update) | async-done | bytes 819216 | tf_op jit(solution)/shard_map/psum | solution.py:99
  1107.5 5.7 multiply_reduce_fusion
  1113.8 0.9 subtract_convert_fusion
  (108 shorter events, 6.8 us)
Async XLA Ops:
  8.0 5.1 copy-start.19
  8.0 264.3 %all-reduce.5.cloned.1.call-start = ((), (), s32[]{:S(2)}) async-start(), calls=%async_computation.2 | async-start | bytes 819200 | tf_op jit(solution)/shard_map/psum | solution.py:9
  10.9 273.6 %all-gather.3.cloned.1.call-start = ((), (), s32[]{:S(2)}) async-start(), calls=%async_computation.3 | async-start | bytes 4128768 | tf_op jit(solution)/shard_map/all_gather | solution.py:89
  13.0 1.0 copy-start
  13.0 544.4 %all-reduce.7.cloned.1.call-start = ((), (), s32[]{:S(2)}) async-start(), calls=%async_computation.5 | async-start | bytes 1638400 | tf_op jit(solution)/shard_map/psum | solution.py:99
  19.3 3.4 copy-start.21
  22.8 3.4 copy-start.22
  22.8 3.4 copy-start.23
  22.8 3.4 copy-start.24
  276.3 2.3 copy-start.7
  279.9 1.2 copy-start.1
  279.9 2.1 copy-start.11
  281.1 0.8 copy-start.13
  281.1 0.9 copy-start.15
  290.9 3.8 copy-start.5
  290.9 3.8 copy-start.8
  294.6 3.0 copy-start.2
  298.0 2.2 copy-start.14
  298.0 2.2 copy-start.16
  300.0 257.5 %reduce-scatter.3.cloned.1.call-start = ((), (), s32[]{:S(2)}) async-start(), calls=%async_computation.4 | async-start | bytes 7372800 | tf_op jit(solution)/shard_map/reduce_scatter | solution.py:97
  308.0 510.8 %all-reduce.9.cloned.1.call-start = ((), (), s32[]{:S(2)}) async-start(), calls=%async_computation.6 | async-start | bytes 819200 | tf_op jit(solution)/shard_map/psum | solution.py:9
  313.3 249.6 %copy-start.20 = (f32[256]{0:T(256)S(1)}, f32[256]{0:T(256)}, u32[]{:S(2)}) copy-start(f32[256]{0:T(256)} %param.18) | copy-start | bytes 3076
  313.3 249.6 %copy-start.4 = (bf16[256,800]{0,1:T(8,128)(2,1)S(1)}, bf16[256,800]{0,1:T(8,128)(2,1)}, u32[]{:S(2)}) copy-start(bf16[256,800]{0,1:T(8,128)(2,1)} %param.17) | copy-start | bytes 1228804
  564.0 264.8 %all-gather.5.cloned.1.call-start = ((), (), s32[]{:S(2)}) async-start(), calls=%async_computation.7 | async-start | bytes 3686400 | tf_op jit(solution)/shard_map/all_gather | solution.py:89
  564.6 542.9 %all-reduce.11.cloned.1.call-start = ((), (), s32[]{:S(2)}) async-start(), calls=%async_computation.9 | async-start | bytes 1638400 | tf_op jit(solution)/shard_map/psum | solution.py:99
  567.0 2.7 copy-start.3
  824.6 1.6 copy-start.12
  825.1 3.8 copy-start.17
  841.2 3.7 copy-start.6
  841.2 3.7 copy-start.9
  848.1 2.3 copy-start.18
  850.1 257.5 %reduce-scatter.5.cloned.1.call-start = ((), (), s32[]{:S(2)}) async-start(), calls=%async_computation.8 | async-start | bytes 7372800 | tf_op jit(solution)/shard_map/reduce_scatter | solution.py:97
  858.1 1.6 copy-start.10
Sparse Core Ops, SparseCore 0:
  12.0 260.1 all-reduce.4
  300.1 257.3 all-reduce.6
  564.2 254.5 all-reduce.8
  850.2 257.2 all-reduce.10
Sparse Core Ops, SparseCore 1:
  13.3 51.3 all-gather.2
  308.1 72.5 reduce-scatter.2
  566.3 53.8 all-gather.4
  858.2 72.5 reduce-scatter.4
where the time goes:
time: 1120 us
  waiting for transfers between devices  979 us (87%)
  local copies, waits for them, and re-layouts  59 us (5%)
  matrix products  49.2 us (4%)
  between operations  17.3 us (2%)
  other arithmetic  16.4 us (1%)
    psum x2, waiting for transfers between devices, broadcast(): return lax.psum(kept, axis)  490 us
    psum x2, waiting for transfers between devices, per_device(): source_total = lax.psum(source_part, 'member')  489 us
    dot_general x6, matrix products, scatter_rows(): lax.dot_general(onehot, values, (((0,), (0,)), ((), ())), precision=lax.P...  30.4 us
  transfers between devices with their start and end apart: 8, of which 4 were waited for; matrix products, arithmetic and copies ran while one was open for 6% of the time, Pallas kernels for 0%

commit v1 on v0

--- a/solution.py
+++ b/solution.py
@@ -6,7 +6,7 @@
 
 def broadcast(value, axis, source):
     kept = jnp.where(lax.axis_index(axis) == source, value, 0).astype(value.dtype)
-    return lax.psum(kept, axis)
+    return jnp.sum(jax.lax.all_gather(kept, axis), 0)
 
 
 def complex_query(source, rel):

time: 1120 us -> 1160 us (1.036); the launches traced: 1120 us -> 1150 us
  local copies, waits for them, and re-layouts: 59 us -> 80.5 us
  other arithmetic: 16.4 us -> 31.9 us
    psum x2 -> x0, waiting for transfers between devices: 490 us -> none  [broadcast(): return lax.psum(kept, axis)]
    all_gather x0 -> x2, waiting for transfers between devices: none -> 255 us  [broadcast(): return jnp.sum(jax.lax.all_gather(kept, axis), 0)]
    reduce_scatter x2, waiting for transfers between devices: 0.01 us -> 151 us  [per_device(): lax.psum_scatter(spread, 'group', scatter_dimension=0, tiled=True)]
    all_gather x2, waiting for transfers between devices: 0.01 us -> 82.1 us  [per_device(): whole = lax.all_gather(table, 'group', axis=0, tiled=True)]
    unnamed x52 -> x38, local copies, waits for them, and re-layouts: 10.7 us -> 33.8 us
    reduce_sum x0 -> x2, other arithmetic: none -> 21.5 us  [broadcast(): return jnp.sum(jax.lax.all_gather(kept, axis), 0)]
  transfers between devices with their start and end apart: 8 -> 8, of which waited for: 4 -> 8; matrix products, arithmetic and copies ran while one was open for 6% -> 6% of each run, Pallas kernels for 0% -> 0%
where the time goes in v1:
time: 1160 us; the launch traced here: 1150 us
  waiting for transfers between devices  973 us (84%)
  local copies, waits for them, and re-layouts  80.5 us (7%)
  matrix products  43.7 us (4%)
  other arithmetic  31.9 us (3%)
  between operations  16.4 us (1%)
    psum x2, waiting for transfers between devices, per_device(): source_total = lax.psum(source_part, 'member')  485 us
    all_gather x2, waiting for transfers between devices, broadcast(): return jnp.sum(jax.lax.all_gather(kept, axis), 0)  255 us
    reduce_scatter x2, waiting for transfers between devices, per_device(): lax.psum_scatter(spread, 'group', scatter_dimension=0, tiled=True)  151 us
    all_gather x2, waiting for transfers between devices, per_device(): whole = lax.all_gather(table, 'group', axis=0, tiled=True)  82.1 us
    unnamed x38, local copies, waits for them, and re-layouts  33.8 us
    dot_general x6, matrix products, scatter_rows(): lax.dot_general(onehot, values, (((0,), (0,)), ((), ())), precision=lax.P...  30.6 us
  transfers between devices with their start and end apart: 8, of which 8 were waited for; matrix products, arithmetic and copies ran while one was open for 6% of the time, Pallas kernels for 0%

profile of v1, /device:TPU:16, one launch (start us, length us, event | category | flops | bytes accessed | tf_op | source)
XLA Modules:
  0.0 1146.4 jit_solution(9447415240493280149)
XLA Ops:
  7.2 2.0 copy.27
  9.3 1.4 constant_dynamic-slice_fusion.1
  12.3 5.3 gather_fusion.3
  17.5 3.4 copy.25
  21.0 2.1 gather_fusion.1
  23.1 1.2 copy.26
  24.5 36.0 %all-gather.7.cloned.1.call-done = bf16[2048,800]{1,0:T(8,128)(2,1)} async-done(((bf16[256,800]{1,0:T(8,128)(2,1)}), bf16[2048,800]{1,0:T(8,128)(2,1)}) %all-gather.7.cloned.1.call-update) | async-done | bytes 3276816 | tf_op jit(solution)/shard_map/all_gather | solution.py:89
  60.5 5.0 gather_fusion.2
  65.5 1.3 copy.28
  66.8 131.0 %all-gather.11.cloned.1.call-done = bf16[8192,800]{0,1:T(8,128)(2,1)} async-done(((bf16[256,800]{0,1:T(8,128)(2,1)}), bf16[8192,800]{0,1:T(8,128)(2,1)}) %all-gather.11.cloned.1.call-update) | async-done | bytes 13107216 | tf_op jit(solution)/shard_map/all_gather | solution.py:9
  197.8 12.5 %copy.37 = bf16[100,8,32,256]{3,2,1,0:T(8,128)(2,1)} copy(bf16[100,8,32,256]{3,1,2,0:T(8,128)(2,1)} %bitcast.24) | data formatting | bytes 26214400
  210.2 10.8 bitcast_reduce_fusion.1
  221.2 3.1 gather_fusion
  224.3 2.3 copy.24
  226.6 1.4 select_convert_fusion.2
  229.7 1.3 fusion.44
  231.4 1.4 fusion.7
  233.1 1.9 fusion.10
  235.1 7.7 fusion
  243.5 4.7 fusion.38
  248.2 242.1 %all-reduce.3.cloned.1.call-done = f32[256,800]{0,1:T(8,128)} async-done(((f32[256,800]{0,1:T(8,128)}), f32[256,800]{0,1:T(8,128)}) %all-reduce.3.cloned.1.call-update) | async-done | bytes 819216 | tf_op jit(solution)/shard_map/psum | solution.py:99
  490.4 75.4 %reduce-scatter.3.cloned.1.call-done = f32[256,800]{0,1:T(8,128)} async-done(((f32[2048,800]{0,1:T(8,128)}), f32[256,800]{0,1:T(8,128)}) %reduce-scatter.3.cloned.1.call-update) | async-done | bytes 819216 | tf_op jit(solution)/shard_map/reduce_scatter | solution.py:97
  565.7 5.4 multiply_reduce_fusion.1
  571.2 1.1 broadcast_select_fusion.8
  573.1 2.1 gather_fusion.5
  575.2 1.2 copy.33
  576.6 1.3 select_convert_fusion
  578.1 5.3 gather_fusion.7
  583.4 46.1 %all-gather.9.cloned.1.call-done = bf16[2048,800]{0,1:T(8,128)(2,1)} async-done(((bf16[256,800]{0,1:T(8,128)(2,1)}), bf16[2048,800]{0,1:T(8,128)(2,1)}) %all-gather.9.cloned.1.call-update) | async-done | bytes 3276816 | tf_op jit(solution)/shard_map/all_gather | solution.py:89
  629.4 6.0 copy.34
  635.4 5.0 gather_fusion.6
  640.4 1.2 copy.35
  641.7 124.3 %all-gather.13.cloned.1.call-done = bf16[8192,800]{0,1:T(8,128)(2,1)} async-done(((bf16[256,800]{0,1:T(8,128)(2,1)}), bf16[8192,800]{0,1:T(8,128)(2,1)}) %all-gather.13.cloned.1.call-update) | async-done | bytes 13107216 | tf_op jit(solution)/shard_map/all_gather | solution.py:9
  766.0 12.5 %copy.38 = bf16[100,8,32,256]{3,2,1,0:T(8,128)(2,1)} copy(bf16[100,8,32,256]{3,1,2,0:T(8,128)(2,1)} %bitcast.25) | data formatting | bytes 26214400
  778.5 10.8 bitcast_reduce_fusion
  789.5 2.3 gather_fusion.4
  791.8 1.3 copy.31
  793.0 1.3 select_convert_fusion.1
  796.0 1.3 fusion.45
  797.7 1.4 fusion.9
  799.5 1.9 fusion.14
  801.5 8.0 fusion.1
  809.5 1.6 copy-done.8
  811.0 3.1 fusion.37
  814.1 242.6 %all-reduce.5.cloned.1.call-done = f32[256,800]{0,1:T(8,128)} async-done(((f32[256,800]{0,1:T(8,128)}), f32[256,800]{0,1:T(8,128)}) %all-reduce.5.cloned.1.call-update) | async-done | bytes 819216 | tf_op jit(solution)/shard_map/psum | solution.py:99
  1056.7 75.3 %reduce-scatter.5.cloned.1.call-done = f32[256,800]{0,1:T(8,128)} async-done(((f32[2048,800]{0,1:T(8,128)}), f32[256,800]{0,1:T(8,128)}) %reduce-scatter.5.cloned.1.call-update) | async-done | bytes 819216 | tf_op jit(solution)/shard_map/reduce_scatter | solution.py:97
  1132.0 5.7 multiply_reduce_fusion
  1138.3 0.9 subtract_convert_fusion
  (96 shorter events, 8.4 us)
Async XLA Ops:
  7.2 5.0 copy-start.11
  7.2 53.3 %all-gather.7.cloned.1.call-start = ((), (), s32[]{:S(2)}) async-start(), calls=%async_computation.2 | async-start | bytes 4128768 | tf_op jit(solution)/shard_map/all_gather | solution.py:89
  9.2 3.1 copy-start
  9.2 188.5 %all-gather.11.cloned.1.call-start = ((), (), s32[]{:S(2)}) async-start(), calls=%async_computation.8 | async-start | bytes 13516800 | tf_op jit(solution)/shard_map/all_gather | solution.py:9
  12.2 478.2 %all-reduce.3.cloned.1.call-start = ((), (), s32[]{:S(2)}) async-start(), calls=%async_computation.4 | async-start | bytes 1638400 | tf_op jit(solution)/shard_map/psum | solution.py:99
  17.5 3.4 copy-start.13
  21.0 3.3 copy-start.14
  21.0 3.4 copy-start.15
  21.0 3.4 copy-start.16
  224.3 2.3 copy-start.5
  227.9 1.1 copy-start.3
  228.0 1.7 copy-start.9
  231.0 1.8 copy-start.6
  235.1 330.7 %reduce-scatter.3.cloned.1.call-start = ((), (), s32[]{:S(2)}) async-start(), calls=%async_computation.3 | async-start | bytes 7372800 | tf_op jit(solution)/shard_map/reduce_scatter | solution.py:97
  242.9 386.6 %all-gather.9.cloned.1.call-start = ((), (), s32[]{:S(2)}) async-start(), calls=%async_computation.5 | async-start | bytes 3686400 | tf_op jit(solution)/shard_map/all_gather | solution.py:89
  248.2 322.9 %copy-start.12 = (f32[256]{0:T(256)S(1)}, f32[256]{0:T(256)}, u32[]{:S(2)}) copy-start(f32[256]{0:T(256)} %param.18) | copy-start | bytes 3076
  248.2 323.0 %copy-start.2 = (bf16[256,800]{0,1:T(8,128)(2,1)S(1)}, bf16[256,800]{0,1:T(8,128)(2,1)}, u32[]{:S(2)}) copy-start(bf16[256,800]{0,1:T(8,128)(2,1)} %param.17) | copy-start | bytes 1228804
  572.3 193.7 %all-gather.13.cloned.1.call-start = ((), (), s32[]{:S(2)}) async-start(), calls=%async_computation.9 | async-start | bytes 13516800 | tf_op jit(solution)/shard_map/all_gather | solution.py:9
  572.9 483.8 %all-reduce.5.cloned.1.call-start = ((), (), s32[]{:S(2)}) async-start(), calls=%async_computation.7 | async-start | bytes 1638400 | tf_op jit(solution)/shard_map/psum | solution.py:99
  575.2 2.6 copy-start.1
  794.3 1.1 copy-start.4
  794.3 1.7 copy-start.10
  797.3 1.8 copy-start.7
  801.4 330.6 %reduce-scatter.5.cloned.1.call-start = ((), (), s32[]{:S(2)}) async-start(), calls=%async_computation.6 | async-start | bytes 7372800 | tf_op jit(solution)/shard_map/reduce_scatter | solution.py:97
  809.4 1.6 copy-start.8
Sparse Core Ops, SparseCore 0:
  9.8 50.6 all-gather.6
  63.6 134.0 all-gather.10
  235.2 255.1 all-reduce.2
  493.0 72.7 reduce-scatter.2
  572.4 56.9 all-gather.8
  632.8 133.2 all-gather.12
  801.5 255.1 all-reduce.4
  1059.3 72.6 reduce-scatter.4
